TPU v7x, 32 devices: a whole 2x2x4 slice. The times are simulated.
32 devices in a mesh: row: 4 (over y, core), col: 8 (over z, x).
Axes of the slice: x: 2, y: 2, z: 4, core: 2. Of those that a mesh axis runs over, the one named last changes fastest.
Arguments:
- left: bfloat16 [128, 8192], P('col', 'row'), may hold values from -6 to 6
- right: bfloat16 [128, 8192], P('row', 'col'), may hold values from -6 to 6
- proj: bfloat16 [1024, 128], replicated, may hold values from -2 to 2
- bias: float32 [128], replicated, may hold values from -1 to 1
- pair_grad: bfloat16 [256, 256, 128], P('row', 'col'), may hold values from -0.1875 to 0.1875
Outputs:
- pair_out: bfloat16 [256, 256, 128], P('row', 'col')
- left_grad: float32 [128, 8192], P('col', 'row')
- right_grad: float32 [128, 8192], P('row', 'col')
- proj_grad: float32 [1024, 128], replicated
All inputs are finite; a program needn't handle non-finite values.
Results may differ from a plain program's by a relative error of at most 0.0056.
Values may be sent and summed in bfloat16 or wider, within the bound.
A program may use at most 128 MiB of HBM per device.

v0:
```python
import jax
import jax.numpy as jnp
from jax import lax
from jax.sharding import PartitionSpec as P

CH = 32
PAIR = 128
SEQS = 128
OUTER = 1024


def shards(left, right, proj, bias, pair_grad):
    left_all = lax.all_gather(left, "col", axis=0, tiled=True)
    right_all = lax.all_gather(right, "row", axis=0, tiled=True)
    seq_count = left_all.shape[0]
    rows_here = left_all.shape[1] // CH
    cols_here = right_all.shape[1] // CH
    left_cube = left_all.reshape(seq_count, rows_here, CH)
    right_cube = right_all.reshape(seq_count, cols_here, CH)
    square = (
        jnp.einsum("sic,sje->ijce", left_cube, right_cube, preferred_element_type=jnp.float32)
        / SEQS
    )
    outers = square.astype(jnp.bfloat16).reshape(rows_here * cols_here, OUTER)
    preact = jnp.dot(outers, proj, preferred_element_type=jnp.float32) + bias
    active = jnp.maximum(preact, 0.0)
    pair_out = (active * active).astype(jnp.bfloat16).reshape(rows_here, cols_here, PAIR)
    grad_pre = (
        pair_grad.reshape(rows_here * cols_here, PAIR).astype(jnp.float32) * 2.0 * active
    ).astype(jnp.bfloat16)
    weight_term = lax.dot_general(
        outers, grad_pre, (((0,), (0,)), ((), ())), preferred_element_type=jnp.float32
    )
    proj_grad = lax.psum(weight_term, ("row", "col"))
    grad_outer = jnp.dot(grad_pre, proj.T, preferred_element_type=jnp.float32).astype(jnp.bfloat16)
    grad_cube = grad_outer.reshape(rows_here, cols_here, CH, CH)
    left_whole = (
        jnp.einsum("ijce,sje->sic", grad_cube, right_cube, preferred_element_type=jnp.float32)
        / SEQS
    )
    right_whole = (
        jnp.einsum("ijce,sic->sje", grad_cube, left_cube, preferred_element_type=jnp.float32) / SEQS
    )
    left_grad = lax.psum_scatter(
        left_whole.reshape(seq_count, rows_here * CH), "col", scatter_dimension=0, tiled=True
    )
    right_grad = lax.psum_scatter(
        right_whole.reshape(seq_count, cols_here * CH), "row", scatter_dimension=0, tiled=True
    )
    return (pair_out, left_grad, right_grad, proj_grad)


def solution(mesh):
    return jax.shard_map(
        shards,
        mesh=mesh,
        in_specs=(P("col", "row"), P("row", "col"), P(), P(), P("row", "col", None)),
        out_specs=(P("row", "col", None), P("col", "row"), P("row", "col"), P()),
        check_vma=False,
    )
```

profile of v0, /device:TPU:0, one launch (start us, length us, event | category | flops | bytes accessed | tf_op | source)
XLA Modules:
  0.0 248.4 jit_solution(3948851120335303654)
XLA Ops:
  8.0 0.0 copy-start
  8.0 0.0 all-reduce.2.cloned.1.call-start
  8.1 33.4 %all_gather.7 = bf16[128,2048]{1,0:T(8,128)(2,1)S(1)} all-gather(bf16[16,2048]{1,0:T(8,128)(2,1)} %param.5), channel_id=1, replica_groups=mesh['row'=4,'col'=8] {'col'}, dimensions={0}, use_global_device_ids=true | all-gather | bytes 589824 | tf_op jit(solution)/shard_map/all_gather | solution.py:13
  41.4 0.3 copy.26
  41.7 6.0 %all_gather.6 = bf16[128,1024]{1,0:T(8,128)(2,1)S(1)} all-gather(bf16[32,1024]{1,0:T(8,128)(2,1)} %param.6), channel_id=1, replica_groups=mesh['row'=4,'col'=8] {'row'}, dimensions={0}, use_global_device_ids=true | all-gather | bytes 327680 | tf_op jit(solution)/shard_map/all_gather | solution.py:14
  47.7 0.2 copy.25
  47.9 5.6 %fusion = bf16[64,32,32,32]{0,3,2,1:T(8,128)(2,1)} fusion(bf16[128,32,32,1]{0,2,3,1:T(8,128)(2,1)S(1)} %bitcast.50, bf16[128,64,32]{0,2,1:T(8,128)(2,1)S(1)} %bitcast.48), kind=kOutput, calls=%fused_computation.1 | convolution fusion | flops 541065216 | bytes 4980736 | tf_op jit(solution)/shard_map/sic,sje->ijce/dot_general | solution.py:21
  53.5 24.6 %copy.28 = bf16[64,32,32,32]{3,2,1,0:T(8,128)(2,1)} copy(bf16[64,32,32,32]{0,3,2,1:T(8,128)(2,1)} %fusion) | data formatting | bytes 8388608 | tf_op jit(solution)/shard_map/convert_element_type | solution.py:24
  78.1 0.0 copy-start.2
  78.1 0.0 copy-start.3
  78.1 23.3 %reshape.36 = bf16[2048,1024]{1,0:T(8,128)(2,1)} reshape(bf16[64,32,32,32]{3,2,1,0:T(8,128)(2,1)} %copy.28) | data formatting | bytes 8388608 | tf_op jit(solution)/shard_map/reshape | solution.py:24
  101.4 0.0 copy-done.2
  101.4 0.0 copy-start.1
  101.4 0.1 convert_multiply_fusion
  101.6 0.0 copy-done
  101.6 0.0 copy-done.3
  101.6 4.4 %fusion.4 = (bf16[2048,128]{1,0:T(8,128)(2,1)S(1)}, bf16[2048,128]{1,0:T(8,128)(2,1)}) fusion(f32[64,32,128]{2,1,0:T(8,128)S(1)} %convert_multiply_fusion, f32[128]{0:T(128)S(1)} %copy-done.3, bf16[2048,1024]{1,0:T(8,128)(2,1)} %reshape.36, bf16[1024,128]{1,0:T(8,128)(2,1)S(1)} %copy-done), kind=kOutput, calls=%fused_computation.10 | convolution fusion | flops 538443776 | bytes 6554112 | tf_op jit(solution)/shard_map/dot_general | solution.py:25
  106.0 0.0 copy-done.1
  106.0 2.1 fusion.7
  108.1 0.0 all-reduce.2.cloned.1.call-update
  108.1 0.2 reduce-scatter.5.cloned.1.call-start
  108.3 3.2 %convolution_convert_fusion = bf16[2048,1024]{1,0:T(8,128)(2,1)} fusion(bf16[2048,128]{1,0:T(8,128)(2,1)S(1)} %get-tuple-element.4, bf16[1024,128]{1,0:T(8,128)(2,1)S(1)} %copy-done), kind=kOutput, calls=%fused_computation.2 | convolution fusion | flops 538968064 | bytes 4980736 | tf_op jit(solution)/shard_map/dot_general | solution.py:35
  111.5 20.3 %reshape.38 = bf16[64,32,32,32]{3,2,1,0:T(8,128)(2,1)} reshape(bf16[2048,1024]{1,0:T(8,128)(2,1)} %convolution_convert_fusion) | data formatting | bytes 8388608 | tf_op jit(solution)/shard_map/reshape | solution.py:36
  131.9 10.3 %fusion.3 = f32[32,32,128]{2,1,0:T(8,128)S(1)} fusion(bf16[64,32,32,32]{3,2,1,0:T(8,128)(2,1)} %reshape.38, bf16[128,64,32,1]{0,2,3,1:T(8,128)(2,1)S(1)} %bitcast.49), kind=kOutput, calls=%fused_computation.8 | convolution fusion | flops 537001984 | bytes 5242880 | tf_op jit(solution)/shard_map/ijce,sic->sje/dot_general | solution.py:42
  142.2 1.0 copy.31
  143.2 0.0 reduce-scatter.5.cloned.1.call-update
  143.2 0.0 reduce-scatter.3.cloned.1.call-start
  143.3 9.1 %fusion.2 = f32[64,32,128]{2,1,0:T(8,128)S(1)} fusion(bf16[64,32,32,32]{3,2,1,0:T(8,128)(2,1)} %reshape.38, bf16[128,32,32,1]{0,2,1,3:T(8,128)(2,1)S(1)} %bitcast.51), kind=kOutput, calls=%fused_computation.6 | convolution fusion | flops 537133056 | bytes 5505024 | tf_op jit(solution)/shard_map/ijce,sje->sic/dot_general | solution.py:38
  152.4 1.3 copy.29
  153.7 0.0 reduce-scatter.3.cloned.1.call-update
  153.8 85.4 %all-reduce.2.cloned.1.call-done = f32[1024,128]{1,0:T(8,128)} async-done(((f32[1024,128]{1,0:T(8,128)}), f32[1024,128]{1,0:T(8,128)}) %all-reduce.2.cloned.1.call-update) | async-done | bytes 524304 | tf_op jit(solution)/shard_map/psum | solution.py:34
  239.1 1.9 copy.41
  (2 shorter events, 0.0 us)
Async XLA Ops:
  8.0 93.6 %copy-start = (bf16[1024,128]{1,0:T(8,128)(2,1)S(1)}, bf16[1024,128]{1,0:T(8,128)(2,1)}, u32[]{:S(2)}) copy-start(bf16[1024,128]{1,0:T(8,128)(2,1)} %param.7) | copy-start | bytes 786436
  8.0 231.1 %all-reduce.2.cloned.1.call-start = ((), (), s32[]{:S(2)}) async-start(), calls=%async_computation.4 | async-start | bytes 1048576 | tf_op jit(solution)/shard_map/psum | solution.py:34
  78.1 23.3 %copy-start.2 = (bf16[64,32,128]{2,1,0:T(8,128)(2,1)S(1)}, bf16[64,32,128]{2,1,0:T(8,128)(2,1)}, u32[]{:S(2)}) copy-start(bf16[64,32,128]{2,1,0:T(8,128)(2,1)} %param.9) | copy-start | bytes 1572868
  78.1 23.5 %copy-start.3 = (f32[128]{0:T(128)S(1)}, f32[128]{0:T(128)}, u32[]{:S(2)}) copy-start(f32[128]{0:T(128)} %param.8) | copy-start | bytes 1540
  101.4 4.5 %copy-start.1 = (bf16[2048,1024]{1,0:T(8,128)(2,1)S(1)}, bf16[2048,1024]{1,0:T(8,128)(2,1)}, u32[]{:S(2)}) copy-start(bf16[2048,1024]{1,0:T(8,128)(2,1)} %reshape.36) | copy-start | bytes 12582916
  108.1 131.0 %reduce-scatter.5.cloned.1.call-start = ((), (), s32[]{:S(2)}) async-start(), calls=%async_computation.3 | async-start | bytes 655360 | tf_op jit(solution)/shard_map/reduce_scatter | solution.py:47
  143.2 95.9 %reduce-scatter.3.cloned.1.call-start = ((), (), s32[]{:S(2)}) async-start(), calls=%async_computation.2 | async-start | bytes 1179648 | tf_op jit(solution)/shard_map/reduce_scatter | solution.py:44
Sparse Core Ops, SparseCore 0:
  108.2 130.8 all-reduce.1
Sparse Core Ops, SparseCore 1:
  143.3 22.7 reduce-scatter.4
  169.9 64.3 reduce-scatter.2
where the time goes:
time: 250 us; the launch traced here: 248 us
  waiting for transfers between devices  85.4 us (34%)
  local copies, waits for them, and re-layouts  72.9 us (29%)
  blocking collectives  39.4 us (16%)
  matrix products  34.8 us (14%)
  between operations  15.5 us (6%)
    psum x1, waiting for transfers between devices, shards(): proj_grad = lax.psum(weight_term, ('row', 'col'))  85.4 us
    all_gather x1, blocking collectives, shards(): left_all = lax.all_gather(left, 'col', axis=0, tiled=True)  33.4 us
    convert_element_type x1, local copies, waits for them, and re-layouts, shards(): outers = square.astype(jnp.bfloat16).reshape(rows_here * cols_here, OUTER)  24.6 us
    reshape x1, local copies, waits for them, and re-layouts, shards(): outers = square.astype(jnp.bfloat16).reshape(rows_here * cols_here, OUTER)  23.3 us
    reshape x1, local copies, waits for them, and re-layouts, shards(): grad_cube = grad_outer.reshape(rows_here, cols_here, CH, CH)  20.3 us
    dot_general x1, matrix products, shards(): jnp.einsum('ijce,sic->sje', grad_cube, left_cube, preferred_element_type=...  10.3 us
    dot_general x1, matrix products, shards(): jnp.einsum('ijce,sje->sic', grad_cube, right_cube, preferred_element_type...  9.14 us
    all_gather x1, blocking collectives, shards(): right_all = lax.all_gather(right, 'row', axis=0, tiled=True)  5.99 us
  transfers between devices with their start and end apart: 3, of which 1 were waited for; matrix products, arithmetic and copies ran while one was open for 18% of the time, Pallas kernels for 0%

commit v1 on v0

--- a/solution.py
+++ b/solution.py
@@ -31,7 +31,7 @@
     weight_term = lax.dot_general(
         outers, grad_pre, (((0,), (0,)), ((), ())), preferred_element_type=jnp.float32
     )
-    proj_grad = lax.psum(weight_term, ("row", "col"))
+    proj_grad = lax.psum(lax.psum(weight_term, "col"), "row")
     grad_outer = jnp.dot(grad_pre, proj.T, preferred_element_type=jnp.float32).astype(jnp.bfloat16)
     grad_cube = grad_outer.reshape(rows_here, cols_here, CH, CH)
     left_whole = (

time: 250 us -> 319 us (1.28)
  waiting for transfers between devices: 85.4 us -> 156 us
    reduce_scatter x1, waiting for transfers between devices: 0.01 us -> 68 us  [shards(): lax.psum_scatter(left_whole.reshape(seq_count, rows_here * CH), 'col', sc...]
    reduce_scatter x1, waiting for transfers between devices: 0.01 us -> 24.8 us  [shards(): lax.psum_scatter(right_whole.reshape(seq_count, cols_here * CH), 'row', s...]
    psum x1 -> x2, waiting for transfers between devices: 85.4 us -> 63.2 us  [shards(): proj_grad = lax.psum(lax.psum(weight_term, 'col'), 'row')]
  transfers between devices with their start and end apart: 3 -> 4, of which waited for: 1 -> 4; matrix products, arithmetic and copies ran while one was open for 18% -> 14% of each run, Pallas kernels for 0% -> 0%
where the time goes in v1:
time: 319 us; the launch traced here: 317 us
  waiting for transfers between devices  156 us (49%)
  local copies, waits for them, and re-layouts  72.9 us (23%)
  blocking collectives  39.4 us (12%)
  matrix products  34.8 us (11%)
  between operations  13.8 us (4%)
    reduce_scatter x1, waiting for transfers between devices, shards(): lax.psum_scatter(left_whole.reshape(seq_count, rows_here * CH), 'col', sc...  68 us
    psum x2, waiting for transfers between devices, shards(): proj_grad = lax.psum(lax.psum(weight_term, 'col'), 'row')  63.2 us
    all_gather x1, blocking collectives, shards(): left_all = lax.all_gather(left, 'col', axis=0, tiled=True)  33.4 us
    reduce_scatter x1, waiting for transfers between devices, shards(): lax.psum_scatter(right_whole.reshape(seq_count, cols_here * CH), 'row', s...  24.8 us
    convert_element_type x1, local copies, waits for them, and re-layouts, shards(): outers = square.astype(jnp.bfloat16).reshape(rows_here * cols_here, OUTER)  24.6 us
    reshape x1, local copies, waits for them, and re-layouts, shards(): outers = square.astype(jnp.bfloat16).reshape(rows_here * cols_here, OUTER)  23.3 us
    reshape x1, local copies, waits for them, and re-layouts, shards(): grad_cube = grad_outer.reshape(rows_here, cols_here, CH, CH)  20.3 us
    dot_general x1, matrix products, shards(): jnp.einsum('ijce,sic->sje', grad_cube, left_cube, preferred_element_type=...  10.3 us
  transfers between devices with their start and end apart: 4, of which 4 were waited for; matrix products, arithmetic and copies ran while one was open for 14% of the time, Pallas kernels for 0%

profile of v1, /device:TPU:0, one launch (start us, length us, event | category | flops | bytes accessed | tf_op | source)
XLA Modules:
  0.0 317.3 jit_solution(17756645603200646269)
XLA Ops:
  7.2 0.0 copy-start
  7.2 0.0 all-reduce.3.cloned.1.call-start
  7.2 33.4 %all_gather.7 = bf16[128,2048]{1,0:T(8,128)(2,1)S(1)} all-gather(bf16[16,2048]{1,0:T(8,128)(2,1)} %param.5), channel_id=1, replica_groups=mesh['row'=4,'col'=8] {'col'}, dimensions={0}, use_global_device_ids=true | all-gather | bytes 589824 | tf_op jit(solution)/shard_map/all_gather | solution.py:13
  40.6 0.3 copy.26
  40.9 6.0 %all_gather.6 = bf16[128,1024]{1,0:T(8,128)(2,1)S(1)} all-gather(bf16[32,1024]{1,0:T(8,128)(2,1)} %param.6), channel_id=1, replica_groups=mesh['row'=4,'col'=8] {'row'}, dimensions={0}, use_global_device_ids=true | all-gather | bytes 327680 | tf_op jit(solution)/shard_map/all_gather | solution.py:14
  46.9 0.2 copy.25
  47.1 5.6 %fusion = bf16[64,32,32,32]{0,3,2,1:T(8,128)(2,1)} fusion(bf16[128,32,32,1]{0,2,3,1:T(8,128)(2,1)S(1)} %bitcast.50, bf16[128,64,32]{0,2,1:T(8,128)(2,1)S(1)} %bitcast.48), kind=kOutput, calls=%fused_computation.1 | convolution fusion | flops 541065216 | bytes 4980736 | tf_op jit(solution)/shard_map/sic,sje->ijce/dot_general | solution.py:21
  52.7 24.6 %copy.28 = bf16[64,32,32,32]{3,2,1,0:T(8,128)(2,1)} copy(bf16[64,32,32,32]{0,3,2,1:T(8,128)(2,1)} %fusion) | data formatting | bytes 8388608 | tf_op jit(solution)/shard_map/convert_element_type | solution.py:24
  77.3 23.3 %reshape.36 = bf16[2048,1024]{1,0:T(8,128)(2,1)} reshape(bf16[64,32,32,32]{3,2,1,0:T(8,128)(2,1)} %copy.28) | data formatting | bytes 8388608 | tf_op jit(solution)/shard_map/reshape | solution.py:24
  100.6 0.0 copy-done.2
  100.6 0.1 convert_multiply_fusion
  100.7 4.4 %fusion.4 = (bf16[2048,128]{1,0:T(8,128)(2,1)S(1)}, bf16[2048,128]{1,0:T(8,128)(2,1)}) fusion(f32[64,32,128]{2,1,0:T(8,128)S(1)} %convert_multiply_fusion, f32[128]{0:T(128)S(1)} %copy-done.3, bf16[2048,1024]{1,0:T(8,128)(2,1)} %reshape.36, bf16[1024,128]{1,0:T(8,128)(2,1)S(1)} %copy-done), kind=kOutput, calls=%fused_computation.10 | convolution fusion | flops 538443776 | bytes 6554112 | tf_op jit(solution)/shard_map/dot_general | solution.py:25
  105.1 0.0 copy-done.1
  105.1 2.1 fusion.7
  107.2 0.0 all-reduce.3.cloned.1.call-update
  107.3 0.0 all-reduce.5.cloned.1.call-start
  107.3 3.2 %convolution_convert_fusion = bf16[2048,1024]{1,0:T(8,128)(2,1)} fusion(bf16[2048,128]{1,0:T(8,128)(2,1)S(1)} %get-tuple-element.4, bf16[1024,128]{1,0:T(8,128)(2,1)S(1)} %copy-done), kind=kOutput, calls=%fused_computation.2 | convolution fusion | flops 538968064 | bytes 4980736 | tf_op jit(solution)/shard_map/dot_general | solution.py:35
  110.5 20.3 %reshape.38 = bf16[64,32,32,32]{3,2,1,0:T(8,128)(2,1)} reshape(bf16[2048,1024]{1,0:T(8,128)(2,1)} %convolution_convert_fusion) | data formatting | bytes 8388608 | tf_op jit(solution)/shard_map/reshape | solution.py:36
  130.8 50.4 %all-reduce.3.cloned.1.call-done = f32[1024,128]{1,0:T(8,128)} async-done(((f32[1024,128]{1,0:T(8,128)}), f32[1024,128]{1,0:T(8,128)}) %all-reduce.3.cloned.1.call-update) | async-done | bytes 524304 | tf_op jit(solution)/shard_map/psum | solution.py:34
  181.2 0.0 all-reduce.5.cloned.1.call-update
  181.2 0.2 reduce-scatter.5.cloned.1.call-start
  181.4 10.3 %fusion.3 = f32[32,32,128]{2,1,0:T(8,128)S(1)} fusion(bf16[64,32,32,32]{3,2,1,0:T(8,128)(2,1)} %reshape.38, bf16[128,64,32,1]{0,2,3,1:T(8,128)(2,1)S(1)} %bitcast.49), kind=kOutput, calls=%fused_computation.8 | convolution fusion | flops 537001984 | bytes 5242880 | tf_op jit(solution)/shard_map/ijce,sic->sje/dot_general | solution.py:42
  191.7 1.0 copy.31
  192.7 0.0 reduce-scatter.5.cloned.1.call-update
  192.7 0.0 reduce-scatter.3.cloned.1.call-start
  192.8 9.2 %fusion.2 = f32[64,32,128]{2,1,0:T(8,128)S(1)} fusion(bf16[64,32,32,32]{3,2,1,0:T(8,128)(2,1)} %reshape.38, bf16[128,32,32,1]{0,2,1,3:T(8,128)(2,1)S(1)} %bitcast.51), kind=kOutput, calls=%fused_computation.6 | convolution fusion | flops 537133056 | bytes 5505024 | tf_op jit(solution)/shard_map/ijce,sje->sic/dot_general | solution.py:38
  202.0 1.3 copy.29
  203.3 0.0 reduce-scatter.3.cloned.1.call-update
  203.3 12.8 %all-reduce.5.cloned.1.call-done = f32[1024,128]{1,0:T(8,128)} async-done(((f32[1024,128]{1,0:T(8,128)}), f32[1024,128]{1,0:T(8,128)}) %all-reduce.5.cloned.1.call-update) | async-done | bytes 524304 | tf_op jit(solution)/shard_map/psum | solution.py:34
  216.1 24.8 %reduce-scatter.5.cloned.1.call-done = f32[32,1024]{1,0:T(8,128)} async-done(((f32[128,1024]{1,0:T(8,128)}), f32[32,1024]{1,0:T(8,128)}) %reduce-scatter.5.cloned.1.call-update) | async-done | bytes 131088 | tf_op jit(solution)/shard_map/reduce_scatter | solution.py:47
  241.0 68.0 %reduce-scatter.3.cloned.1.call-done = f32[16,2048]{1,0:T(8,128)} async-done(((f32[128,2048]{1,0:T(8,128)}), f32[16,2048]{1,0:T(8,128)}) %reduce-scatter.3.cloned.1.call-update) | async-done | bytes 131088 | tf_op jit(solution)/shard_map/reduce_scatter | solution.py:44
  308.9 1.9 copy.42
  (5 shorter events, 0.0 us)
Async XLA Ops:
  7.2 93.6 %copy-start = (bf16[1024,128]{1,0:T(8,128)(2,1)S(1)}, bf16[1024,128]{1,0:T(8,128)(2,1)}, u32[]{:S(2)}) copy-start(bf16[1024,128]{1,0:T(8,128)(2,1)} %param.7) | copy-start | bytes 786436
  7.2 174.0 %all-reduce.3.cloned.1.call-start = ((), (), s32[]{:S(2)}) async-start(), calls=%async_computation.4 | async-start | bytes 1048576 | tf_op jit(solution)/shard_map/psum | solution.py:34
  77.3 23.3 %copy-start.2 = (bf16[64,32,128]{2,1,0:T(8,128)(2,1)S(1)}, bf16[64,32,128]{2,1,0:T(8,128)(2,1)}, u32[]{:S(2)}) copy-start(bf16[64,32,128]{2,1,0:T(8,128)(2,1)} %param.9) | copy-start | bytes 1572868
  77.3 23.5 %copy-start.3 = (f32[128]{0:T(128)S(1)}, f32[128]{0:T(128)}, u32[]{:S(2)}) copy-start(f32[128]{0:T(128)} %param.8) | copy-start | bytes 1540
  100.6 4.5 %copy-start.1 = (bf16[2048,1024]{1,0:T(8,128)(2,1)S(1)}, bf16[2048,1024]{1,0:T(8,128)(2,1)}, u32[]{:S(2)}) copy-start(bf16[2048,1024]{1,0:T(8,128)(2,1)} %reshape.36) | copy-start | bytes 12582916
  107.3 108.9 %all-reduce.5.cloned.1.call-start = ((), (), s32[]{:S(2)}) async-start(), calls=%async_computation.5 | async-start | bytes 1048576 | tf_op jit(solution)/shard_map/psum | solution.py:34
  181.2 59.8 %reduce-scatter.5.cloned.1.call-start = ((), (), s32[]{:S(2)}) async-start(), calls=%async_computation.3 | async-start | bytes 655360 | tf_op jit(solution)/shard_map/reduce_scatter | solution.py:47
  192.7 116.2 %reduce-scatter.3.cloned.1.call-start = ((), (), s32[]{:S(2)}) async-start(), calls=%async_computation.2 | async-start | bytes 1179648 | tf_op jit(solution)/shard_map/reduce_scatter | solution.py:44
Sparse Core Ops, SparseCore 0:
  107.4 73.7 all-reduce.2
  183.5 32.5 all-reduce.4
  219.2 21.7 reduce-scatter.4
  244.8 64.0 reduce-scatter.2
